TPU v7x, 128 devices: a whole 4x4x4 slice. The times are simulated.
128 devices in a mesh: loop: 16 (over y_lo, z, core), red: 8 (over y_hi, x).
Axes of the slice: x: 4, y: 4 (y_hi: 2, y_lo: 2; y = y_hi * 2 + y_lo), z: 4, core: 2. Of those that a mesh axis runs over, the one named last changes fastest.
Arguments:
- query_ids: int32 [512], replicated, may hold values from 0 to 8191
- layer_index: int32 [1], replicated, may hold values from 0 to 3
- gradient: bfloat16 [8192, 28672], P('loop', 'red'), may hold values from -6 to 6
- out_basis: bfloat16 [8192, 8192], P('loop'), may hold values from -0.0625 to 0.0625
- in_basis: bfloat16 [28672, 28672], P('red', 'loop'), may hold values from -0.03125 to 0.03125
- out_eigen: float32 [4, 8192], replicated, may hold values from 0.2 to 2
- in_eigen: float32 [4, 28672], P(None, 'loop'), may hold values from 0.2 to 2
Outputs:
- preconditioned: bfloat16 [512, 28672], P('loop', 'red')
All inputs are finite; a program needn't handle non-finite values.
Results may differ from a plain program's by a relative error of at most 0.0055.
Values may be sent and summed in bfloat16 or wider, within the bound.
No kernel may reach another device: no remote copies, remote signals or barrier semaphores. Data moves between devices by JAX's collectives and lax.ppermute only.
A program may use at most 128 MiB of HBM per device.

v0:
```python
import jax
import jax.numpy as jnp
from jax import lax
from jax.sharding import PartitionSpec as P

damping = 0.05


def per_device(query_ids, layer_index, gradient, out_basis, in_basis, out_eigen, in_eigen):
    selected = jnp.take(out_basis, query_ids, axis=1)
    local_rows = lax.dot_general(
        selected, gradient, (((0,), (0,)), ((), ())), preferred_element_type=jnp.float32
    )
    rows_w = lax.psum(local_rows, "loop").astype(jnp.bfloat16)
    eigen_rows = jnp.take(jnp.take(out_eigen, layer_index, axis=0)[0], query_ids)
    eigen_cols = jnp.take(in_eigen, layer_index, axis=0)[0]
    local_rot = jnp.dot(rows_w, in_basis, preferred_element_type=jnp.float32)
    rotated = lax.psum(local_rot, "red")
    scaled = (rotated / (eigen_rows[:, None] * eigen_cols[None, :] + damping)).astype(jnp.bfloat16)
    result = lax.psum_scatter(
        lax.dot_general(
            scaled, in_basis, (((1,), (1,)), ((), ())), preferred_element_type=jnp.float32
        ),
        "loop",
        scatter_dimension=0,
        tiled=True,
    )
    return result.astype(jnp.bfloat16)


def solution(mesh):
    return jax.shard_map(
        per_device,
        mesh=mesh,
        in_specs=(
            P(),
            P(),
            P("loop", "red"),
            P("loop", None),
            P("red", "loop"),
            P(),
            P(None, "loop"),
        ),
        out_specs=P("loop", "red"),
        check_vma=False,
    )
```

profile of v0, /device:TPU:4, one launch (start us, length us, event | category | flops | bytes accessed | tf_op | source)
XLA Modules:
  0.0 341.5 jit_solution(16668026155570244711)
XLA Ops:
  6.5 0.0 all-reduce.3.cloned.1.call-start
  7.2 0.7 compare_select_fusion
  7.9 0.9 broadcast_select_fusion
  8.8 3.1 gather_fusion.1
  12.0 0.7 broadcast_select_fusion.2
  12.7 11.9 %copy.9 = bf16[512,8192]{0,1:T(8,128)(2,1)} copy(bf16[512,8192]{1,0:T(8,128)(2,1)} %param.10) | data formatting | bytes 16777216 | tf_op args[3]
  24.6 6.4 %gather_fusion = bf16[512,512]{1,0:T(8,128)(2,1)S(1)} fusion(bf16[512,8192]{0,1:T(8,128)(2,1)} %copy.9, s32[1024]{0:T(1024)S(1)} %pad_clamp_fusion), kind=kCustom, calls=%fused_computation | custom fusion | bytes 1050624 | tf_op jit(solution)/shard_map/jit(_take)/gather | solution.py:10
  31.1 7.1 %fusion.6 = f32[512,3584]{1,0:T(8,128)} fusion(bf16[512,3584]{1,0:T(8,128)(2,1)} %param.9, bf16[512,512]{1,0:T(8,128)(2,1)S(1)} %gather_fusion, pred[512]{0:T(512)(128)(4,1)S(1)} %get-tuple-element.28), kind=kOutput, calls=%fused_computation.9 | convolution fusion | flops 1879310336 | bytes 11534848 | tf_op jit(solution)/shard_map/dot_general | solution.py:11
  38.2 93.1 %all-reduce.4 = bf16[512,3584]{1,0:T(8,128)(2,1)} all-reduce(f32[512,3584]{1,0:T(8,128)} %fusion.6), channel_id=1, replica_groups=mesh['loop'=16,'red'=8] {'loop'}, use_global_device_ids=true, to_apply=%region_0.1 | all-reduce | flops 1835008 | bytes 11010048 | tf_op jit(solution)/shard_map/psum | solution.py:14
  131.4 13.4 %fusion.13 = f32[512,1792]{1,0:T(8,128)} fusion(bf16[512,3584]{1,0:T(8,128)(2,1)} %all-reduce.4, bf16[3584,1792]{1,0:T(8,128)(2,1)} %param.11), kind=kOutput, calls=%fused_computation.22 | convolution fusion | flops 6576668672 | bytes 20185088 | tf_op jit(solution)/shard_map/dot_general | solution.py:17
  144.8 0.0 all-reduce.3.cloned.1.call-update
  144.8 0.0 reduce-scatter.2.cloned.1.call-start
  144.8 0.8 fusion.10
  145.6 99.3 %all-reduce.3.cloned.1.call-done = f32[512,1792]{1,0:T(8,128)} async-done(((f32[512,1792]{1,0:T(8,128)}), f32[512,1792]{1,0:T(8,128)}) %all-reduce.3.cloned.1.call-update) | async-done | bytes 3670032 | tf_op jit(solution)/shard_map/psum | solution.py:18
  244.9 12.9 %fusion.2 = f32[512,3584]{1,0:T(8,128)} fusion(bf16[3584,1792]{1,0:T(8,128)(2,1)} %param.11, f32[512,1792]{1,0:T(8,128)} %all-reduce.3.cloned.1.call-done, f32[1792]{0:T(1024)S(1)} %fusion.10, f32[512]{0:T(512)S(1)} %get-tuple-element.27), kind=kOutput, calls=%fused_computation.5 | convolution fusion | flops 6580338688 | bytes 23864320 | tf_op jit(solution)/shard_map/dot_general | solution.py:21
  257.8 0.0 reduce-scatter.2.cloned.1.call-update
  257.9 75.1 %reduce-scatter.2.cloned.1.call-done = f32[32,3584]{1,0:T(8,128)} async-done(((f32[512,3584]{1,0:T(8,128)}), f32[32,3584]{1,0:T(8,128)}) %reduce-scatter.2.cloned.1.call-update) | async-done | bytes 458768 | tf_op jit(solution)/shard_map/reduce_scatter | solution.py:20
  332.9 1.7 convert_element_type.11
  (1 shorter events, 0.0 us)
Async XLA Ops:
  6.5 238.4 %all-reduce.3.cloned.1.call-start = ((), (), s32[]{:S(2)}) async-start(), calls=%async_computation.1 | async-start | bytes 7340032 | tf_op jit(solution)/shard_map/psum | solution.py:18
  144.8 188.2 %reduce-scatter.2.cloned.1.call-start = ((), (), s32[]{:S(2)}) async-start(), calls=%async_computation.2 | async-start | bytes 7798784 | tf_op jit(solution)/shard_map/reduce_scatter | solution.py:20
Sparse Core Ops, SparseCore 0:
  144.9 99.9 all-reduce.2
  258.0 74.9 reduce-scatter.1
where the time goes:
time: 342 us
  waiting for transfers between devices  174 us (51%)
  blocking collectives  93.1 us (27%)
  matrix products  33.5 us (10%)
  local copies, waits for them, and re-layouts  21.5 us (6%)
  between operations  14.1 us (4%)
  other arithmetic  4.84 us (1%)
    psum x1, waiting for transfers between devices, per_device(): rotated = lax.psum(local_rot, 'red')  99.3 us
    psum x1, blocking collectives, per_device(): rows_w = lax.psum(local_rows, 'loop').astype(jnp.bfloat16)  93.1 us
    reduce_scatter x1, waiting for transfers between devices, per_device(): lax.psum_scatter(lax.dot_general(scaled, in_basis, (((1,), (1,)), ((), ()...  75.1 us
    dot_general x1, matrix products, per_device(): local_rot = jnp.dot(rows_w, in_basis, preferred_element_type=jnp.float32)  13.4 us
    dot_general x1, matrix products, per_device(): lax.dot_general(scaled, in_basis, (((1,), (1,)), ((), ())), preferred_ele...  12.9 us
    unnamed x1, local copies, waits for them, and re-layouts  11.9 us
    dot_general x1, matrix products, per_device(): lax.dot_general(selected, gradient, (((0,), (0,)), ((), ())), preferred_e...  7.14 us
  transfers between devices with their start and end apart: 2, of which 2 were waited for; matrix products, arithmetic and copies ran while one was open for 0% of the time, Pallas kernels for 0%

commit v1 on v0

--- a/solution.py
+++ b/solution.py
@@ -15,7 +15,7 @@
     eigen_rows = jnp.take(jnp.take(out_eigen, layer_index, axis=0)[0], query_ids)
     eigen_cols = jnp.take(in_eigen, layer_index, axis=0)[0]
     local_rot = jnp.dot(rows_w, in_basis, preferred_element_type=jnp.float32)
-    rotated = lax.psum(local_rot, "red")
+    rotated = jnp.sum(jax.lax.all_gather(local_rot, axis_name="red"), axis=0)
     scaled = (rotated / (eigen_rows[:, None] * eigen_cols[None, :] + damping)).astype(jnp.bfloat16)
     result = lax.psum_scatter(
         lax.dot_general(

time: 342 us -> 552 us (1.61)
  waiting for transfers between devices: 174 us -> 371 us
  other arithmetic: 4.84 us -> 17.6 us
    all_gather x0 -> x1, waiting for transfers between devices: none -> 298 us  [per_device(): rotated = jnp.sum(jax.lax.all_gather(local_rot, axis_name='red'), axis=0)]
    psum x1 -> x0, waiting for transfers between devices: 99.3 us -> none  [per_device(): rotated = lax.psum(local_rot, 'red')]
    reduce_sum x0 -> x1, other arithmetic: none -> 12.8 us  [per_device(): rotated = jnp.sum(jax.lax.all_gather(local_rot, axis_name='red'), axis=0)]
where the time goes in v1:
time: 552 us; the launch traced here: 551 us
  waiting for transfers between devices  371 us (67%)
  blocking collectives  93.1 us (17%)
  matrix products  33.5 us (6%)
  local copies, waits for them, and re-layouts  21.5 us (4%)
  other arithmetic  17.6 us (3%)
  between operations  14.1 us (3%)
    all_gather x1, waiting for transfers between devices, per_device(): rotated = jnp.sum(jax.lax.all_gather(local_rot, axis_name='red'), axis=0)  298 us
    psum x1, blocking collectives, per_device(): rows_w = lax.psum(local_rows, 'loop').astype(jnp.bfloat16)  93.1 us
    reduce_scatter x1, waiting for transfers between devices, per_device(): lax.psum_scatter(lax.dot_general(scaled, in_basis, (((1,), (1,)), ((), ()...  72.5 us
    dot_general x1, matrix products, per_device(): local_rot = jnp.dot(rows_w, in_basis, preferred_element_type=jnp.float32)  13.4 us
    dot_general x1, matrix products, per_device(): lax.dot_general(scaled, in_basis, (((1,), (1,)), ((), ())), preferred_ele...  12.9 us
    reduce_sum x1, other arithmetic, per_device(): rotated = jnp.sum(jax.lax.all_gather(local_rot, axis_name='red'), axis=0)  12.8 us
    unnamed x1, local copies, waits for them, and re-layouts  11.9 us
  transfers between devices with their start and end apart: 2, of which 2 were waited for; matrix products, arithmetic and copies ran while one was open for 0% of the time, Pallas kernels for 0%

profile of v1, /device:TPU:4, one launch (start us, length us, event | category | flops | bytes accessed | tf_op | source)
XLA Modules:
  0.0 550.7 jit_solution(10373813082227248028)
XLA Ops:
  6.5 0.0 all-gather.3.cloned.1.call-start
  7.2 0.7 compare_select_fusion
  7.9 0.9 broadcast_select_fusion
  8.8 3.1 gather_fusion.1
  12.0 0.7 broadcast_select_fusion.2
  12.7 11.9 %copy.9 = bf16[512,8192]{0,1:T(8,128)(2,1)} copy(bf16[512,8192]{1,0:T(8,128)(2,1)} %param.10) | data formatting | bytes 16777216 | tf_op args[3]
  24.6 6.4 %gather_fusion = bf16[512,512]{1,0:T(8,128)(2,1)S(1)} fusion(bf16[512,8192]{0,1:T(8,128)(2,1)} %copy.9, s32[1024]{0:T(1024)S(1)} %pad_clamp_fusion), kind=kCustom, calls=%fused_computation | custom fusion | bytes 1050624 | tf_op jit(solution)/shard_map/jit(_take)/gather | solution.py:10
  31.1 7.1 %fusion.6 = f32[512,3584]{1,0:T(8,128)} fusion(bf16[512,3584]{1,0:T(8,128)(2,1)} %param.9, bf16[512,512]{1,0:T(8,128)(2,1)S(1)} %gather_fusion, pred[512]{0:T(512)(128)(4,1)S(1)} %get-tuple-element.28), kind=kOutput, calls=%fused_computation.9 | convolution fusion | flops 1879310336 | bytes 11534848 | tf_op jit(solution)/shard_map/dot_general | solution.py:11
  38.2 93.1 %all-reduce.1 = bf16[512,3584]{1,0:T(8,128)(2,1)} all-reduce(f32[512,3584]{1,0:T(8,128)} %fusion.6), channel_id=1, replica_groups=mesh['loop'=16,'red'=8] {'loop'}, use_global_device_ids=true, to_apply=%region_0.1 | all-reduce | flops 1835008 | bytes 11010048 | tf_op jit(solution)/shard_map/psum | solution.py:14
  131.4 13.4 %fusion.13 = f32[512,1792]{1,0:T(8,128)} fusion(bf16[512,3584]{1,0:T(8,128)(2,1)} %all-reduce.1, bf16[3584,1792]{1,0:T(8,128)(2,1)} %param.11), kind=kOutput, calls=%fused_computation.22 | convolution fusion | flops 6576668672 | bytes 20185088 | tf_op jit(solution)/shard_map/dot_general | solution.py:17
  144.8 0.0 all-gather.3.cloned.1.call-update
  144.8 0.0 reduce-scatter.2.cloned.1.call-start
  144.9 0.8 fusion.10
  145.7 298.2 %all-gather.3.cloned.1.call-done = f32[4096,1792]{1,0:T(8,128)} async-done(((f32[512,1792]{1,0:T(8,128)}), f32[4096,1792]{1,0:T(8,128)}) %all-gather.3.cloned.1.call-update) | async-done | bytes 29360144 | tf_op jit(solution)/shard_map/all_gather | solution.py:18
  443.9 12.8 %reduce_sum.9 = f32[512,1792]{1,0:T(8,128)} reduce(f32[8,512,1792]{2,1,0:T(8,128)} %bitcast.9, f32[]{:T(128)} %constant.54.clone.1), dimensions={0}, to_apply=%region_1.2 | reduce | flops 6422528 | bytes 33030148 | tf_op jit(solution)/shard_map/reduce_sum | solution.py:18
  456.6 12.9 %fusion.2 = f32[512,3584]{1,0:T(8,128)} fusion(bf16[3584,1792]{1,0:T(8,128)(2,1)} %param.11, f32[512,1792]{1,0:T(8,128)} %reduce_sum.9, f32[1792]{0:T(1024)S(1)} %fusion.10, f32[512]{0:T(512)S(1)} %get-tuple-element.27), kind=kOutput, calls=%fused_computation.5 | convolution fusion | flops 6580338688 | bytes 23864320 | tf_op jit(solution)/shard_map/dot_general | solution.py:21
  469.6 0.0 reduce-scatter.2.cloned.1.call-update
  469.6 72.5 %reduce-scatter.2.cloned.1.call-done = f32[32,3584]{1,0:T(8,128)} async-done(((f32[512,3584]{1,0:T(8,128)}), f32[32,3584]{1,0:T(8,128)}) %reduce-scatter.2.cloned.1.call-update) | async-done | bytes 458768 | tf_op jit(solution)/shard_map/reduce_scatter | solution.py:20
  542.1 1.7 convert_element_type.11
  (1 shorter events, 0.0 us)
Async XLA Ops:
  6.5 437.3 %all-gather.3.cloned.1.call-start = ((), (), s32[]{:S(2)}) async-start(), calls=%async_computation.2 | async-start | bytes 33030144 | tf_op jit(solution)/shard_map/all_gather | solution.py:18
  144.8 397.3 %reduce-scatter.2.cloned.1.call-start = ((), (), s32[]{:S(2)}) async-start(), calls=%async_computation.1 | async-start | bytes 7798784 | tf_op jit(solution)/shard_map/reduce_scatter | solution.py:20
Sparse Core Ops, SparseCore 0:
  144.9 298.8 all-gather.2
  469.7 72.3 reduce-scatter.1
